TPU v7x, 512 devices: a whole 4x4x16 slice. The times are simulated.
512 devices in a mesh: sub: 128 (over z, x, core), blk: 4 (over y).
Axes of the slice: x: 4, y: 4, z: 16, core: 2. Of those that a mesh axis runs over, the one named last changes fastest.
Arguments:
- factor: bfloat16 [256, 2048, 2048], P('sub', None, 'blk'), may hold values from -0.125 to 0.125
- samples: bfloat16 [256, 2048, 128], P('sub', 'blk'), may hold values from -6 to 6
- diagonal: bfloat16 [256, 128, 16], P('sub'), may hold values from 0.25 to 1
- coupling: bfloat16 [256, 64, 2048], P('sub', 'blk'), may hold values from -0.125 to 0.125
- blocks: int32 [256], P('sub'), may hold values from 80 to 128, as said below
- peer_device: int32 [256, 128], P('sub'), may hold values from 0 to 127, as said below
- peer_lane: int32 [256, 128], P('sub'), may hold values from 0 to 1, as said below
- owns_face: int32 [256, 128], P('sub'), may hold values from 0 to 1, as said below
Outputs:
- interior: bfloat16 [256, 64, 128], P('sub', 'blk')
Inputs may be any that keep to these rules, and one draw needn't show every extreme that they name: Each subdomain's interface has blocks face blocks; over the subdomains of one index of sub they sum to 208. `peer_device`: live slots are matched in pairs of partners as the statement says, one owning side each; each index of sub owns 104 faces and holds 104 faces owned elsewhere; all faces between two indices of sub are owned by the same one of them; slots that are not live hold 0. Live slots of one index of sub with the same peer_device and the same owns_face have different peer_lane; slots that are not live hold 0. `owns_face`: slots that are not live hold 0.
All inputs are finite; a program needn't handle non-finite values.
Results may differ from a plain program's by a relative error of at most 0.013.
Values may be sent and summed in bfloat16 or wider, within the bound.
No kernel may reach another device: no remote copies, remote signals or barrier semaphores. Data moves between devices by JAX's collectives and lax.ppermute only.
A program may use at most 64 MiB of HBM per device.

v0:
```python
import jax
import jax.numpy as jnp
from jax import lax
from jax.experimental import pallas as pl
from jax.experimental.pallas import tpu as pltpu
from jax.sharding import PartitionSpec as P


BF16 = jnp.bfloat16
F32 = jnp.float32
LANES = 2
BLK = 4
TILE = 16
PART = TILE // BLK
MEMBERS = LANES * PART
PAY = MEMBERS + 2
FIRST = 48
FACES = 208

VMEM = pltpu.VMEM
TN = (((0,), (0,)), ((), ()))
NT = (((1,), (1,)), ((), ()))


def targets(blocks, device_ref, lane_ref, s, peers):
    shape = (8, device_ref.shape[1])
    place = jnp.broadcast_to(lane_ref[s : s + 1] * peers + device_ref[s : s + 1], shape)
    live = lax.broadcasted_iota(jnp.int32, shape, 1) < blocks[s]
    return jnp.where(live, place, -1)


def one_hot(target, positions):
    shape = (positions, target.shape[1])
    hit = lax.broadcasted_iota(jnp.int32, shape, 0) == jnp.broadcast_to(target[:1], shape)
    return jnp.where(hit, 1.0, 0.0).astype(BF16)


def products(blocks, shards, factor, offsets, accs, ready):
    subs = len(accs)
    for s in range(subs):
        for shard, j in shards:
            rows = offsets[j] + lax.broadcasted_iota(jnp.int32, shard.shape[1:], 0)
            part = jnp.where(rows < blocks[s] * TILE, shard[s].astype(F32), 0.0).astype(BF16)
            ready(s, j)
            piece = lax.dot_general(
                part,
                factor[s, pl.ds(offsets[j], shard.shape[1]), :],
                TN,
                preferred_element_type=F32,
            )
            accs[s] = piece if accs[s] is None else accs[s] + piece
    return accs


def row_offsets(here, quarter):
    return [pl.multiple_of(lax.rem(here + j, BLK) * quarter, quarter) for j in range(BLK)]


def first_kernel(blocks, device_ref, lane_ref, diag, d0, factor, fac, acc_ref, diag_ref, sems):
    subs, _, quarter = factor.shape
    here = lax.axis_index("blk")
    offsets = row_offsets(here, quarter)
    copies = {}
    for j in range(BLK):
        for s in range(subs):
            rows = pl.ds(offsets[j], quarter)
            copies[s, j] = pltpu.make_async_copy(
                factor.at[s, rows, :], fac.at[s, rows, :], sems.at[s * BLK + j]
            )
            copies[s, j].start()
    peers, width = diag_ref.shape
    total = jnp.zeros(diag_ref.shape, F32)
    row = lax.broadcasted_iota(jnp.int32, (TILE, width), 0)
    col = lax.broadcasted_iota(jnp.int32, (TILE, width), 1)
    for s in range(subs):
        pick = one_hot(targets(blocks, device_ref, lane_ref, s, peers), peers * LANES)
        for lane in range(LANES):
            low = lane * PART
            hit = (col >= low) & (col < low + PART) & (row == here * PART + col - low)
            spread = jnp.where(hit, 1.0, 0.0).astype(BF16)
            found = lax.dot_general(
                pick[lane * peers : (lane + 1) * peers], diag[s], NT, preferred_element_type=F32
            )
            total += jnp.dot(found.astype(BF16), spread, preferred_element_type=F32)
    diag_ref[...] = total
    accs = products(
        blocks, ((d0, 0),), fac, offsets, [None] * subs, lambda s, j: copies[s, j].wait()
    )
    for s in range(subs):
        acc_ref[s] = accs[s]
        for j in range(1, BLK):
            copies[s, j].wait()


def near_kernel(blocks, d2, d3, acc_ref, fac, out_ref):
    offsets = row_offsets(lax.axis_index("blk"), fac.shape[2])
    accs = products(
        blocks,
        ((d2, 2), (d3, 3)),
        fac,
        offsets,
        [acc_ref[s] for s in range(fac.shape[0])],
        lambda s, j: None,
    )
    for s in range(fac.shape[0]):
        out_ref[s] = accs[s]


def traces_kernel(blocks, d1, acc_ref, fac, c1, c2, c3, o0, o1, o2, o3, wide):
    subs, order, quarter = fac.shape
    here = lax.axis_index("blk")
    offsets = row_offsets(here, quarter)
    accs = products(
        blocks, ((d1, 1),), fac, offsets, [acc_ref[s] for s in range(subs)], lambda s, j: None
    )
    start = jnp.int32(0)
    for s in range(subs):
        cols = offsets[0] + lax.broadcasted_iota(jnp.int32, accs[s].shape, 1)
        reduced = jnp.where(cols < blocks[s] * TILE, accs[s], 0.0).astype(BF16)
        wide[pl.ds(pl.multiple_of(start * TILE, TILE), order), :] = lax.dot_general(
            fac[s], reduced, NT, preferred_element_type=F32
        )
        start = start + blocks[s]
    for j, out in enumerate((o0, o1, o2, o3)):
        part = lax.rem(here + j, BLK)
        for i in range(PART):
            rows = wide[pl.ds(part * PART + i, FACES, stride=TILE), :]
            out[i * FACES : (i + 1) * FACES] = rows.astype(BF16)
    for out, piece in ((o1, c1), (o2, c2), (o3, c3)):
        out[PART * FACES :] = piece[...]


def pack_kernel(
    blocks, device_ref, lane_ref, diag_ref, c0, a0, a2, a1, a3, pay_ref, moved_ref, spread
):
    here = lax.axis_index("blk")
    peers, columns = diag_ref.shape
    positions = peers * LANES
    subs, each = device_ref.shape
    slots = subs * each
    natural = [targets(blocks, device_ref, lane_ref, s, peers) for s in range(subs)]
    empty = jnp.full((8, slots - each), -1, jnp.int32)
    lanes = lax.broadcasted_iota(jnp.int32, (8, slots), 1)
    start = blocks[0]
    compact = jnp.concatenate([natural[0], empty], axis=1)
    for s in range(1, subs):
        turned = pltpu.roll(jnp.concatenate([natural[s], empty], axis=1), start, 1)
        compact = jnp.where(lanes < start, compact, turned)
        start = start + blocks[s]
    pick = one_hot(compact, positions)
    none = jnp.zeros((slots - FACES, columns), BF16)
    for i in range(PART):
        r = slice(i * FACES, (i + 1) * FACES)
        total = (a0[r].astype(F32) + a1[r].astype(F32)) + (a2[r].astype(F32) + a3[r].astype(F32))
        rows = jnp.concatenate([total.astype(BF16), none], axis=0)
        moved = jnp.dot(pick, rows, preferred_element_type=F32)
        for lane in range(LANES):
            spread[pl.ds(lane * PART + i, peers, stride=PAY), :] = moved[
                lane * peers : (lane + 1) * peers
            ]
    spread[pl.ds(MEMBERS, peers, stride=PAY), :] = diag_ref[...]
    spread[pl.ds(MEMBERS + 1, peers, stride=PAY), :] = jnp.zeros_like(diag_ref)
    pay_ref[...] = spread[...].astype(BF16)

    count = PART * FACES
    rows_of = moved_ref.shape[1] // subs
    pieces = (c0[...], a3[count:], a2[count:], a1[count:])
    for s in range(subs):
        pick_s = one_hot(natural[s], positions)
        for i in range(PART):
            low = (i * subs + s) * rows_of
            stacked = jnp.concatenate([c[low : low + rows_of] for c in pieces], axis=0)
            moved = lax.dot_general(stacked, pick_s, NT, preferred_element_type=F32).astype(BF16)
            for j in range(BLK):
                for lane in range(LANES):
                    m = lane * PART + i
                    moved_ref[
                        lax.rem(here + j, BLK),
                        s * rows_of : (s + 1) * rows_of,
                        m * peers : (m + 1) * peers,
                    ] = moved[j * rows_of : (j + 1) * rows_of, lane * peers : (lane + 1) * peers]


def interior_kernel(pay, got, coupling, out, own32, got32, coefs):
    peers = pay.shape[0] // PAY
    own32[...] = pay[...].astype(F32)
    got32[...] = got[...].astype(F32)
    own_diag = own32[pl.ds(MEMBERS, peers, stride=PAY), :]
    both = own_diag + got32[pl.ds(MEMBERS, peers, stride=PAY), :]
    divisor = jnp.where(own_diag > 0.0, both, 1.0)
    for m in range(MEMBERS):
        rows = pl.ds(m, peers, stride=PAY)
        summed = own32[rows, :] + got32[rows, :]
        used = jnp.broadcast_to(own_diag[:, m : m + 1], summed.shape) > 0.0
        below = jnp.broadcast_to(divisor[:, m : m + 1], summed.shape)
        coefs[m * peers : (m + 1) * peers, :] = jnp.where(used, summed / below, 0.0).astype(BF16)
    rows = coupling.shape[0] * coupling.shape[1]
    out[...] = jnp.dot(
        coupling[...].reshape(rows, coupling.shape[2]), coefs[...], preferred_element_type=F32
    ).reshape(out.shape).astype(BF16)


def shift(x, by):
    return lax.ppermute(x, "blk", [(i, (i + by) % BLK) for i in range(BLK)])


def body(factor, samples, diagonal, coupling, blocks, peer_device, peer_lane, owns_face):
    peers = lax.axis_size("sub")
    here = lax.axis_index("blk")
    subs, order, quarter = factor.shape
    slot_count = diagonal.shape[1]
    columns = samples.shape[2]
    inner = coupling.shape[1]
    vmem = pl.BlockSpec(memory_space=VMEM)
    smem = pl.BlockSpec(memory_space=pltpu.SMEM)

    d1 = shift(samples, -1)
    d3 = shift(samples, 1)
    d2 = shift(samples, 2)

    grouped = coupling.reshape(subs, inner, slot_count, BLK, PART).transpose(3, 4, 0, 1, 2)

    def turned(j):
        piece = lax.dynamic_index_in_dim(grouped, lax.rem(here + j, BLK), 0, keepdims=False)
        return piece.reshape(PART * subs * inner, slot_count)

    rows = peers * MEMBERS
    extra = PART * subs * inner
    fac, acc, diag_rows = pl.pallas_call(
        first_kernel,
        out_shape=[
            jax.ShapeDtypeStruct(factor.shape, BF16),
            jax.ShapeDtypeStruct((subs, columns, quarter), F32),
            jax.ShapeDtypeStruct((peers, columns), F32),
        ],
        in_specs=[smem] + [vmem] * 4 + [pl.BlockSpec(memory_space=pltpu.HBM)],
        out_specs=[vmem] * 3,
        scratch_shapes=[pltpu.SemaphoreType.DMA((subs * BLK,))],
        compiler_params=pltpu.CompilerParams(vmem_limit_bytes=FIRST << 20),
        cost_estimate=pl.CostEstimate(
            flops=2 * subs * quarter * quarter * columns, bytes_accessed=4 << 20, transcendentals=0
        ),
        name="first",
    )(blocks, peer_device, peer_lane, diagonal.transpose(0, 2, 1), samples, factor)

    acc = pl.pallas_call(
        near_kernel,
        out_shape=jax.ShapeDtypeStruct((subs, columns, quarter), F32),
        in_specs=[smem] + [vmem] * 4,
        out_specs=vmem,
        compiler_params=pltpu.CompilerParams(vmem_limit_bytes=24 << 20),
        cost_estimate=pl.CostEstimate(
            flops=4 * subs * quarter * quarter * columns, bytes_accessed=4 << 20, transcendentals=0
        ),
        name="near",
    )(blocks, d2, d3, acc, fac)

    count = PART * FACES
    piece = jax.ShapeDtypeStruct((count + extra, columns), BF16)
    o0, o1, o2, o3 = pl.pallas_call(
        traces_kernel,
        out_shape=[jax.ShapeDtypeStruct((count, columns), BF16)] + [piece] * 3,
        in_specs=[smem] + [vmem] * 6,
        out_specs=[vmem] * BLK,
        scratch_shapes=[VMEM((subs * order, columns), F32)],
        compiler_params=pltpu.CompilerParams(vmem_limit_bytes=32 << 20),
        cost_estimate=pl.CostEstimate(
            flops=4 * subs * order * quarter * columns, bytes_accessed=8 << 20, transcendentals=0
        ),
        name="traces",
    )(blocks, d1, acc, fac, turned(1), turned(2), turned(3))

    a2 = shift(o2, 2)
    a1 = shift(o1, 1)
    a3 = shift(o3, -1)

    pay, moved = pl.pallas_call(
        pack_kernel,
        out_shape=[
            jax.ShapeDtypeStruct((peers * PAY, columns), BF16),
            jax.ShapeDtypeStruct((BLK, subs * inner, rows), BF16),
        ],
        in_specs=[smem] + [vmem] * 8,
        out_specs=[vmem] * 2,
        scratch_shapes=[VMEM((peers * PAY, columns), F32)],
        compiler_params=pltpu.CompilerParams(vmem_limit_bytes=16 << 20),
        name="pack",
    )(blocks, peer_device, peer_lane, diag_rows, turned(0), o0, a2, a1, a3)

    got = lax.all_to_all(
        pay.reshape(peers, PAY // 2, 2, columns), "sub", split_axis=0, concat_axis=0, tiled=True
    ).reshape(peers * PAY, columns)

    part = pl.pallas_call(
        interior_kernel,
        out_shape=jax.ShapeDtypeStruct((BLK, subs * inner, columns), BF16),
        in_specs=[vmem] * 3,
        out_specs=vmem,
        scratch_shapes=[
            VMEM((peers * PAY, columns), F32),
            VMEM((peers * PAY, columns), F32),
            VMEM((rows, columns), BF16),
        ],
        compiler_params=pltpu.CompilerParams(vmem_limit_bytes=16 << 20),
        name="interior",
    )(pay, got, moved)

    parts = lax.all_to_all(part, "blk", split_axis=0, concat_axis=0, tiled=True)
    return parts.astype(F32).sum(axis=0).astype(BF16).reshape(subs, inner, columns)


def solution(mesh):
    placed = (
        P("sub", None, "blk"),
        P("sub", "blk", None),
        P("sub", None, None),
        P("sub", "blk", None),
        P("sub"),
        P("sub", None),
        P("sub", None),
        P("sub", None),
    )
    return jax.shard_map(
        body, mesh=mesh, in_specs=placed, out_specs=P("sub", "blk", None), check_vma=False
    )
```

profile of v0, /device:TPU:6, one launch (start us, length us, event | category | flops | bytes accessed | tf_op | source)
XLA Modules:
  0.0 94.9 jit_solution(1246741944525657012)
XLA Ops:
  0.0 0.0 copy-start
  0.0 0.0 copy-start.2
  0.0 0.0 copy-start.4
  0.0 0.0 copy-start.3
  0.0 0.0 copy-start.1
  0.0 3.6 %collective-permute-start.2 = (bf16[2,512,128]{2,1,0:T(8,128)(2,1)}, bf16[2,512,128]{2,1,0:T(8,128)(2,1)S(1)}, u32[]{:S(2)}, u32[]{:S(2)}) collective-permute-start(bf16[2,512,128]{2,1,0:T(8,128)(2,1)} %d0.1), channel_id=1, source_target_pairs={{0,1},{1,2},{2,3},{3,0},{4,5},{5,6},{6,7},{7,4},{8,9},{9,10},{10,1... | collective-permute-start | bytes 786440 | tf_op jit(solution)/shard_map/ppermute | solution.py:204
  3.7 4.8 %collective-permute-start.1 = (bf16[2,512,128]{2,1,0:T(8,128)(2,1)}, bf16[2,512,128]{2,1,0:T(8,128)(2,1)S(1)}, u32[]{:S(2)}, u32[]{:S(2)}) collective-permute-start(bf16[2,512,128]{2,1,0:T(8,128)(2,1)} %d0.1), channel_id=1, source_target_pairs={{0,2},{1,3},{2,0},{3,1},{4,6},{5,7},{6,4},{7,5},{8,10},{9,11},{10,... | collective-permute-start | bytes 786440 | tf_op jit(solution)/shard_map/ppermute | solution.py:204
  8.5 3.3 %collective-permute-start = (bf16[2,512,128]{2,1,0:T(8,128)(2,1)}, bf16[2,512,128]{2,1,0:T(8,128)(2,1)S(1)}, u32[]{:S(2)}, u32[]{:S(2)}) collective-permute-start(bf16[2,512,128]{2,1,0:T(8,128)(2,1)} %d0.1), channel_id=1, source_target_pairs={{0,3},{1,0},{2,1},{3,2},{4,7},{5,4},{6,5},{7,6},{8,11},{9,8},{10,9... | collective-permute-start | bytes 786440 | tf_op jit(solution)/shard_map/ppermute | solution.py:204
  11.8 1.4 %copy.12 = bf16[2,16,2048]{1,2,0:T(8,128)(2,1)S(1)} copy(bf16[2,16,2048]{2,1,0:T(8,128)(2,1)} %param.11) | data formatting | bytes 262144 | tf_op args[3]
  13.2 0.4 dynamic-slice_bitcast_fusion
  13.5 0.1 copy.16
  13.7 0.2 copy.15
  13.8 0.2 copy.14
  14.0 0.0 copy-done
  14.0 0.0 copy-done.2
  14.0 0.0 copy-done.4
  14.0 0.0 copy-done.3
  14.0 0.0 copy-done.1
  14.1 2.8 %first.1 = (bf16[2,2048,512]{2,1,0:T(8,128)(2,1)S(1)}, f32[2,128,512]{2,1,0:T(8,128)S(1)}, f32[128,128]{1,0:T(8,128)S(1)}) custom-call(s32[2]{0:T(128)S(1)} %copy-done.2, s32[2,128]{1,0:T(2,128)S(1)} %copy-done.3, s32[2,128]{1,0:T(2,128)S(1)} %copy-done.4, bf16[2,16,128]{2,1,0:T(8,128)(2,1)S(1)} %bitcast.23, bf16[2,512,128]{2,1,0:T(8,128)(2,1)S(1)} %copy-done, ...), custom_call_target="tpu_custom_call" | custom-call | flops 134217728 | bytes 4194304 | tf_op jit(solution)/shard_map/first/pallas_call | solution.py:229
  16.9 0.0 collective-permute-done.2.d3
  16.9 1.5 %collective-permute-done.1.d2 = bf16[2,512,128]{2,1,0:T(8,128)(2,1)S(1)} collective-permute-done((bf16[2,512,128]{2,1,0:T(8,128)(2,1)}, bf16[2,512,128]{2,1,0:T(8,128)(2,1)S(1)}, u32[]{:S(2)}, u32[]{:S(2)}) %collective-permute-start.1) | collective-permute-done | bytes 262176 | tf_op jit(solution)/shard_map/ppermute | solution.py:204
  18.4 1.1 %near.1.acc_ref = f32[2,128,512]{2,1,0:T(8,128)S(1)} custom-call(s32[2]{0:T(128)S(1)} %copy-done.2, bf16[2,512,128]{2,1,0:T(8,128)(2,1)S(1)} %collective-permute-done.1.d2, bf16[2,512,128]{2,1,0:T(8,128)(2,1)S(1)} %collective-permute-done.2.d3, f32[2,128,512]{2,1,0:T(8,128)S(1)} %get-tuple-element.15.acc_ref, bf16[2,2048,512]{2,1,0:T(8,128)(2,1)S(1)} %get-tuple-element.16.fac), custom_call_target="tpu_custom_call" | custom-call | flops 268435456 | bytes 4194304 | tf_op jit(solution)/shard_map/near/pallas_call | solution.py:246
  19.4 0.3 collective-permute-done.d1
  19.7 2.8 %traces.1 = (bf16[832,128]{1,0:T(8,128)(2,1)S(1)}, bf16[960,128]{1,0:T(8,128)(2,1)S(1)}, bf16[960,128]{1,0:T(8,128)(2,1)S(1)}, bf16[960,128]{1,0:T(8,128)(2,1)S(1)}) custom-call(s32[2]{0:T(128)S(1)} %copy-done.2, bf16[2,512,128]{2,1,0:T(8,128)(2,1)S(1)} %collective-permute-done.d1, f32[2,128,512]{2,1,0:T(8,128)S(1)} %near.1.acc_ref, ...), custom_call_target="tpu_custom_call" | custom-call | flops 1073741824 | bytes 8388608 | tf_op jit(solution)/shard_map/traces/pallas_call | solution.py:260
  22.5 5.1 %collective-permute-start.3 = (bf16[960,128]{1,0:T(8,128)(2,1)S(1)}, bf16[960,128]{1,0:T(8,128)(2,1)S(1)}, u32[]{:S(2)}, u32[]{:S(2)}) collective-permute-start(bf16[960,128]{1,0:T(8,128)(2,1)S(1)} %get-tuple-element.18), channel_id=1, source_target_pairs={{0,2},{1,3},{2,0},{3,1},{4,6},{5,7},{6,4},{7,5},{8,10},{9,11},{10,... | collective-permute-start | bytes 737288 | tf_op jit(solution)/shard_map/ppermute | solution.py:204
  27.6 2.3 %collective-permute-start.4 = (bf16[960,128]{1,0:T(8,128)(2,1)S(1)}, bf16[960,128]{1,0:T(8,128)(2,1)S(1)}, u32[]{:S(2)}, u32[]{:S(2)}) collective-permute-start(bf16[960,128]{1,0:T(8,128)(2,1)S(1)} %get-tuple-element.19), channel_id=1, source_target_pairs={{0,1},{1,2},{2,3},{3,0},{4,5},{5,6},{6,7},{7,4},{8,9},{9,10},{10,1... | collective-permute-start | bytes 737288 | tf_op jit(solution)/shard_map/ppermute | solution.py:204
  29.9 4.8 %collective-permute-start.5 = (bf16[960,128]{1,0:T(8,128)(2,1)S(1)}, bf16[960,128]{1,0:T(8,128)(2,1)S(1)}, u32[]{:S(2)}, u32[]{:S(2)}) collective-permute-start(bf16[960,128]{1,0:T(8,128)(2,1)S(1)} %get-tuple-element.20), channel_id=1, source_target_pairs={{0,3},{1,0},{2,1},{3,2},{4,7},{5,4},{6,5},{7,6},{8,11},{9,8},{10,9... | collective-permute-start | bytes 737288 | tf_op jit(solution)/shard_map/ppermute | solution.py:204
  34.6 0.1 copy.13
  34.8 0.0 collective-permute-done.3.a2
  34.8 3.2 %collective-permute-done.4.a1 = bf16[960,128]{1,0:T(8,128)(2,1)S(1)} collective-permute-done((bf16[960,128]{1,0:T(8,128)(2,1)S(1)}, bf16[960,128]{1,0:T(8,128)(2,1)S(1)}, u32[]{:S(2)}, u32[]{:S(2)}) %collective-permute-start.4) | collective-permute-done | bytes 245792 | tf_op jit(solution)/shard_map/ppermute | solution.py:204
  38.0 0.5 collective-permute-done.5.a3
  38.5 1.1 %pack.1 = (bf16[1280,128]{1,0:T(8,128)(2,1)S(1)}, bf16[4,32,1024]{2,1,0:T(8,128)(2,1)S(1)}) custom-call(s32[2]{0:T(128)S(1)} %copy-done.2, s32[2,128]{1,0:T(2,128)S(1)} %copy-done.3, s32[2,128]{1,0:T(2,128)S(1)} %copy-done.4, f32[128,128]{1,0:T(8,128)S(1)} %get-tuple-element.14.diag_ref, bf16[128,128]{1,0:T(8,128)(2,1)S(1)} %bitcast.22, ...), custom_call_target="tpu_custom_call" | custom-call | tf_op jit(solution)/shard_map/pack/pallas_call | solution.py:277
  39.6 43.9 %all_to_all.10 = bf16[128,5,2,128]{3,2,1,0:T(2,128)(2,1)S(1)} all-to-all(bf16[128,5,2,128]{3,2,1,0:T(2,128)(2,1)S(1)} %bitcast.17), channel_id=1, replica_groups=mesh['sub'=128,'blk'=4] {'sub'}, dimensions={0} | all-to-all | bytes 655360 | tf_op jit(solution)/shard_map/all_to_all | solution.py:290
  83.5 0.6 interior.1
  84.1 10.2 %all_to_all.11 = bf16[4,32,128]{2,1,0:T(8,128)(2,1)S(1)} all-to-all(bf16[4,32,128]{2,1,0:T(8,128)(2,1)S(1)} %interior.1), channel_id=1, replica_groups=mesh['sub'=128,'blk'=4] {'blk'}, dimensions={0} | all-to-all | bytes 65536 | tf_op jit(solution)/shard_map/all_to_all | solution.py:308
  94.3 0.6 reduce_sum.12
Async XLA Ops:
  0.0 14.0 %copy-start = (bf16[2,512,128]{2,1,0:T(8,128)(2,1)S(1)}, bf16[2,512,128]{2,1,0:T(8,128)(2,1)}, u32[]{:S(2)}) copy-start(bf16[2,512,128]{2,1,0:T(8,128)(2,1)} %d0.1) | copy-start | bytes 786436
  0.0 14.0 %copy-start.2 = (s32[2]{0:T(128)S(1)}, s32[2]{0:T(128)}, u32[]{:S(2)}) copy-start(s32[2]{0:T(128)} %blocks.7) | copy-start | bytes 28
  0.0 14.0 %copy-start.4 = (s32[2,128]{1,0:T(2,128)S(1)}, s32[2,128]{1,0:T(2,128)}, u32[]{:S(2)}) copy-start(s32[2,128]{1,0:T(2,128)} %lane_ref.3) | copy-start | bytes 3076
  0.0 14.0 %copy-start.3 = (s32[2,128]{1,0:T(2,128)S(1)}, s32[2,128]{1,0:T(2,128)}, u32[]{:S(2)}) copy-start(s32[2,128]{1,0:T(2,128)} %device_ref.3) | copy-start | bytes 3076
  0.0 14.0 %copy-start.1 = (bf16[2,128,16]{1,2,0:T(8,128)(2,1)S(1)}, bf16[2,128,16]{1,2,0:T(8,128)(2,1)}, u32[]{:S(2)}) copy-start(bf16[2,128,16]{1,2,0:T(8,128)(2,1)} %param.10) | copy-start | bytes 24580
  0.0 16.9 %collective-permute-start.2 = (bf16[2,512,128]{2,1,0:T(8,128)(2,1)}, bf16[2,512,128]{2,1,0:T(8,128)(2,1)S(1)}, u32[]{:S(2)}, u32[]{:S(2)}) collective-permute-start(bf16[2,512,128]{2,1,0:T(8,128)(2,1)} %d0.1), channel_id=1, source_target_pairs={{0,1},{1,2},{2,3},{3,0},{4,5},{5,6},{6,7},{7,4},{8,9},{9,10},{10,1... | collective-permute-start | bytes 786440 | tf_op jit(solution)/shard_map/ppermute | solution.py:204
  3.7 14.7 %collective-permute-start.1 = (bf16[2,512,128]{2,1,0:T(8,128)(2,1)}, bf16[2,512,128]{2,1,0:T(8,128)(2,1)S(1)}, u32[]{:S(2)}, u32[]{:S(2)}) collective-permute-start(bf16[2,512,128]{2,1,0:T(8,128)(2,1)} %d0.1), channel_id=1, source_target_pairs={{0,2},{1,3},{2,0},{3,1},{4,6},{5,7},{6,4},{7,5},{8,10},{9,11},{10,... | collective-permute-start | bytes 786440 | tf_op jit(solution)/shard_map/ppermute | solution.py:204
  8.5 11.2 %collective-permute-start = (bf16[2,512,128]{2,1,0:T(8,128)(2,1)}, bf16[2,512,128]{2,1,0:T(8,128)(2,1)S(1)}, u32[]{:S(2)}, u32[]{:S(2)}) collective-permute-start(bf16[2,512,128]{2,1,0:T(8,128)(2,1)} %d0.1), channel_id=1, source_target_pairs={{0,3},{1,0},{2,1},{3,2},{4,7},{5,4},{6,5},{7,6},{8,11},{9,8},{10,9... | collective-permute-start | bytes 786440 | tf_op jit(solution)/shard_map/ppermute | solution.py:204
  22.5 12.3 %collective-permute-start.3 = (bf16[960,128]{1,0:T(8,128)(2,1)S(1)}, bf16[960,128]{1,0:T(8,128)(2,1)S(1)}, u32[]{:S(2)}, u32[]{:S(2)}) collective-permute-start(bf16[960,128]{1,0:T(8,128)(2,1)S(1)} %get-tuple-element.18), channel_id=1, source_target_pairs={{0,2},{1,3},{2,0},{3,1},{4,6},{5,7},{6,4},{7,5},{8,10},{9,11},{10,... | collective-permute-start | bytes 737288 | tf_op jit(solution)/shard_map/ppermute | solution.py:204
  27.6 10.4 %collective-permute-start.4 = (bf16[960,128]{1,0:T(8,128)(2,1)S(1)}, bf16[960,128]{1,0:T(8,128)(2,1)S(1)}, u32[]{:S(2)}, u32[]{:S(2)}) collective-permute-start(bf16[960,128]{1,0:T(8,128)(2,1)S(1)} %get-tuple-element.19), channel_id=1, source_target_pairs={{0,1},{1,2},{2,3},{3,0},{4,5},{5,6},{6,7},{7,4},{8,9},{9,10},{10,1... | collective-permute-start | bytes 737288 | tf_op jit(solution)/shard_map/ppermute | solution.py:204
  29.9 8.7 %collective-permute-start.5 = (bf16[960,128]{1,0:T(8,128)(2,1)S(1)}, bf16[960,128]{1,0:T(8,128)(2,1)S(1)}, u32[]{:S(2)}, u32[]{:S(2)}) collective-permute-start(bf16[960,128]{1,0:T(8,128)(2,1)S(1)} %get-tuple-element.20), channel_id=1, source_target_pairs={{0,3},{1,0},{2,1},{3,2},{4,7},{5,4},{6,5},{7,6},{8,11},{9,8},{10,9... | collective-permute-start | bytes 737288 | tf_op jit(solution)/shard_map/ppermute | solution.py:204
where the time goes:
time: 95.3 us; the launch traced here: 94.9 us
  blocking collectives  54.1 us (57%)
  starting transfers between devices  23.8 us (25%)
  Pallas kernels  8.33 us (9%)
  waiting for transfers between devices  5.5 us (6%)
  local copies, waits for them, and re-layouts  2.38 us (2%)
    all_to_all x1, blocking collectives, body(): lax.all_to_all(pay.reshape(peers, PAY // 2, 2, columns), 'sub', split_axi...  43.9 us
    ppermute x6, starting transfers between devices, shift(): return lax.ppermute(x, 'blk', [(i, (i + by) % BLK) for i in range(BLK)])  23.8 us
    all_to_all x1, blocking collectives, body(): parts = lax.all_to_all(part, 'blk', split_axis=0, concat_axis=0, tiled=True)  10.2 us
    ppermute x6, waiting for transfers between devices, shift(): return lax.ppermute(x, 'blk', [(i, (i + by) % BLK) for i in range(BLK)])  5.5 us
    pallas_call x1, Pallas kernels, body(): pl.pallas_call(first_kernel, out_shape=[jax.ShapeDtypeStruct(factor.shape...  2.82 us
    pallas_call x1, Pallas kernels, body(): pl.pallas_call(traces_kernel, out_shape=[jax.ShapeDtypeStruct((count, col...  2.78 us
  transfers between devices with their start and end apart: 6, of which 4 were waited for; matrix products, arithmetic and copies ran while one was open for 2% of the time, Pallas kernels for 4%

commit v1 on v0

--- a/solution.py
+++ b/solution.py
@@ -53,7 +53,7 @@
 
 
 def row_offsets(here, quarter):
-    return [pl.multiple_of(lax.rem(here + j, BLK) * quarter, quarter) for j in range(BLK)]
+    return [pl.multiple_of(jnp.bitwise_xor(here, j) * quarter, quarter) for j in range(BLK)]
 
 
 def first_kernel(blocks, device_ref, lane_ref, diag, d0, factor, fac, acc_ref, diag_ref, sems):
@@ -92,11 +92,11 @@
             copies[s, j].wait()
 
 
-def near_kernel(blocks, d2, d3, acc_ref, fac, out_ref):
+def near_kernel(blocks, d2, d1, acc_ref, fac, out_ref):
     offsets = row_offsets(lax.axis_index("blk"), fac.shape[2])
     accs = products(
         blocks,
-        ((d2, 2), (d3, 3)),
+        ((d2, 2), (d1, 1)),
         fac,
         offsets,
         [acc_ref[s] for s in range(fac.shape[0])],
@@ -106,12 +106,12 @@
         out_ref[s] = accs[s]
 
 
-def traces_kernel(blocks, d1, acc_ref, fac, c1, c2, c3, o0, o1, o2, o3, wide):
+def traces_kernel(blocks, d3, acc_ref, fac, c1, c2, c3, o0, o1, o2, o3, wide):
     subs, order, quarter = fac.shape
     here = lax.axis_index("blk")
     offsets = row_offsets(here, quarter)
     accs = products(
-        blocks, ((d1, 1),), fac, offsets, [acc_ref[s] for s in range(subs)], lambda s, j: None
+        blocks, ((d3, 3),), fac, offsets, [acc_ref[s] for s in range(subs)], lambda s, j: None
     )
     start = jnp.int32(0)
     for s in range(subs):
@@ -122,7 +122,7 @@
         )
         start = start + blocks[s]
     for j, out in enumerate((o0, o1, o2, o3)):
-        part = lax.rem(here + j, BLK)
+        part = jnp.bitwise_xor(here, j)
         for i in range(PART):
             rows = wide[pl.ds(part * PART + i, FACES, stride=TILE), :]
             out[i * FACES : (i + 1) * FACES] = rows.astype(BF16)
@@ -164,7 +164,7 @@
 
     count = PART * FACES
     rows_of = moved_ref.shape[1] // subs
-    pieces = (c0[...], a3[count:], a2[count:], a1[count:])
+    pieces = (c0[...], a1[count:], a2[count:], a3[count:])
     for s in range(subs):
         pick_s = one_hot(natural[s], positions)
         for i in range(PART):
@@ -175,7 +175,7 @@
                 for lane in range(LANES):
                     m = lane * PART + i
                     moved_ref[
-                        lax.rem(here + j, BLK),
+                        jnp.bitwise_xor(here, j),
                         s * rows_of : (s + 1) * rows_of,
                         m * peers : (m + 1) * peers,
                     ] = moved[j * rows_of : (j + 1) * rows_of, lane * peers : (lane + 1) * peers]
@@ -200,8 +200,8 @@
     ).reshape(out.shape).astype(BF16)
 
 
-def shift(x, by):
-    return lax.ppermute(x, "blk", [(i, (i + by) % BLK) for i in range(BLK)])
+def swap(x, j):
+    return lax.ppermute(x, "blk", [(i, i ^ j) for i in range(BLK)])
 
 
 def body(factor, samples, diagonal, coupling, blocks, peer_device, peer_lane, owns_face):
@@ -214,14 +214,14 @@
     vmem = pl.BlockSpec(memory_space=VMEM)
     smem = pl.BlockSpec(memory_space=pltpu.SMEM)
 
-    d1 = shift(samples, -1)
-    d3 = shift(samples, 1)
-    d2 = shift(samples, 2)
+    d1 = swap(samples, 1)
+    d3 = swap(samples, 3)
+    d2 = swap(samples, 2)
 
     grouped = coupling.reshape(subs, inner, slot_count, BLK, PART).transpose(3, 4, 0, 1, 2)
 
     def turned(j):
-        piece = lax.dynamic_index_in_dim(grouped, lax.rem(here + j, BLK), 0, keepdims=False)
+        piece = lax.dynamic_index_in_dim(grouped, jnp.bitwise_xor(here, j), 0, keepdims=False)
         return piece.reshape(PART * subs * inner, slot_count)
 
     rows = peers * MEMBERS
@@ -253,7 +253,7 @@
             flops=4 * subs * quarter * quarter * columns, bytes_accessed=4 << 20, transcendentals=0
         ),
         name="near",
-    )(blocks, d2, d3, acc, fac)
+    )(blocks, d2, d1, acc, fac)
 
     count = PART * FACES
     piece = jax.ShapeDtypeStruct((count + extra, columns), BF16)
@@ -268,11 +268,11 @@
             flops=4 * subs * order * quarter * columns, bytes_accessed=8 << 20, transcendentals=0
         ),
         name="traces",
-    )(blocks, d1, acc, fac, turned(1), turned(2), turned(3))
-
-    a2 = shift(o2, 2)
-    a1 = shift(o1, 1)
-    a3 = shift(o3, -1)
+    )(blocks, d3, acc, fac, turned(1), turned(2), turned(3))
+
+    a2 = swap(o2, 2)
+    a1 = swap(o1, 1)
+    a3 = swap(o3, 3)
 
     pay, moved = pl.pallas_call(
         pack_kernel,

time: 95.3 us -> 98 us (1.028)
  waiting for transfers between devices: 5.5 us -> 13.5 us
  starting transfers between devices: 23.8 us -> 20.4 us
  blocking collectives: 54.1 us -> 52.2 us
    ppermute x6, waiting for transfers between devices: 5.5 us -> 13.5 us  [swap(): return lax.ppermute(x, 'blk', [(i, i ^ j) for i in range(BLK)])]
    ppermute x6, starting transfers between devices: 23.8 us -> 20.4 us  [swap(): return lax.ppermute(x, 'blk', [(i, i ^ j) for i in range(BLK)])]
    all_to_all x1, blocking collectives: 10.2 us -> 8.33 us  [body(): parts = lax.all_to_all(part, 'blk', split_axis=0, concat_axis=0, tiled=True)]
  transfers between devices with their start and end apart: 6 -> 6, of which waited for: 4 -> 5; matrix products, arithmetic and copies ran while one was open for 2% -> 2% of each run, Pallas kernels for 4% -> 4%
where the time goes in v1:
time: 98 us; the launch traced here: 97.6 us
  blocking collectives  52.2 us (53%)
  starting transfers between devices  20.4 us (21%)
  waiting for transfers between devices  13.5 us (14%)
  Pallas kernels  8.34 us (9%)
  local copies, waits for them, and re-layouts  2.38 us (2%)
    all_to_all x1, blocking collectives, body(): lax.all_to_all(pay.reshape(peers, PAY // 2, 2, columns), 'sub', split_axi...  43.9 us
    ppermute x6, starting transfers between devices, swap(): return lax.ppermute(x, 'blk', [(i, i ^ j) for i in range(BLK)])  20.4 us
    ppermute x6, waiting for transfers between devices, swap(): return lax.ppermute(x, 'blk', [(i, i ^ j) for i in range(BLK)])  13.5 us
    all_to_all x1, blocking collectives, body(): parts = lax.all_to_all(part, 'blk', split_axis=0, concat_axis=0, tiled=True)  8.33 us
    pallas_call x1, Pallas kernels, body(): pl.pallas_call(first_kernel, out_shape=[jax.ShapeDtypeStruct(factor.shape...  2.81 us
    pallas_call x1, Pallas kernels, body(): pl.pallas_call(traces_kernel, out_shape=[jax.ShapeDtypeStruct((count, col...  2.79 us
  transfers between devices with their start and end apart: 6, of which 5 were waited for; matrix products, arithmetic and copies ran while one was open for 2% of the time, Pallas kernels for 4%

profile of v1, /device:TPU:6, one launch (start us, length us, event | category | flops | bytes accessed | tf_op | source)
XLA Modules:
  0.0 97.6 jit_solution(9249089431329640268)
XLA Ops:
  0.0 0.0 copy-start
  0.0 0.0 copy-start.2
  0.0 0.0 copy-start.4
  0.0 0.0 copy-start.3
  0.0 0.0 copy-start.1
  0.0 3.6 %collective-permute-start.2 = (bf16[2,512,128]{2,1,0:T(8,128)(2,1)}, bf16[2,512,128]{2,1,0:T(8,128)(2,1)S(1)}, u32[]{:S(2)}, u32[]{:S(2)}) collective-permute-start(bf16[2,512,128]{2,1,0:T(8,128)(2,1)} %d0.1), channel_id=1, source_target_pairs={{0,1},{1,0},{2,3},{3,2},{4,5},{5,4},{6,7},{7,6},{8,9},{9,8},{10,11... | collective-permute-start | bytes 786440 | tf_op jit(solution)/shard_map/ppermute | solution.py:204
  3.7 4.8 %collective-permute-start.1 = (bf16[2,512,128]{2,1,0:T(8,128)(2,1)}, bf16[2,512,128]{2,1,0:T(8,128)(2,1)S(1)}, u32[]{:S(2)}, u32[]{:S(2)}) collective-permute-start(bf16[2,512,128]{2,1,0:T(8,128)(2,1)} %d0.1), channel_id=1, source_target_pairs={{0,2},{1,3},{2,0},{3,1},{4,6},{5,7},{6,4},{7,5},{8,10},{9,11},{10,... | collective-permute-start | bytes 786440 | tf_op jit(solution)/shard_map/ppermute | solution.py:204
  8.5 2.1 %collective-permute-start = (bf16[2,512,128]{2,1,0:T(8,128)(2,1)}, bf16[2,512,128]{2,1,0:T(8,128)(2,1)S(1)}, u32[]{:S(2)}, u32[]{:S(2)}) collective-permute-start(bf16[2,512,128]{2,1,0:T(8,128)(2,1)} %d0.1), channel_id=1, source_target_pairs={{0,3},{1,2},{2,1},{3,0},{4,7},{5,6},{6,5},{7,4},{8,11},{9,10},{10,... | collective-permute-start | bytes 786440 | tf_op jit(solution)/shard_map/ppermute | solution.py:204
  10.6 1.4 %copy.12 = bf16[2,16,2048]{1,2,0:T(8,128)(2,1)S(1)} copy(bf16[2,16,2048]{2,1,0:T(8,128)(2,1)} %param.11) | data formatting | bytes 262144 | tf_op args[3]
  12.0 0.4 dynamic-slice_bitcast_fusion
  12.4 0.1 copy.16
  12.5 0.2 copy.15
  12.7 0.2 copy.14
  12.9 0.0 copy-done
  12.9 0.0 copy-done.2
  12.9 0.0 copy-done.4
  12.9 0.0 copy-done.3
  12.9 0.0 copy-done.1
  12.9 2.8 %first.1 = (bf16[2,2048,512]{2,1,0:T(8,128)(2,1)S(1)}, f32[2,128,512]{2,1,0:T(8,128)S(1)}, f32[128,128]{1,0:T(8,128)S(1)}) custom-call(s32[2]{0:T(128)S(1)} %copy-done.2, s32[2,128]{1,0:T(2,128)S(1)} %copy-done.3, s32[2,128]{1,0:T(2,128)S(1)} %copy-done.4, bf16[2,16,128]{2,1,0:T(8,128)(2,1)S(1)} %bitcast.23, bf16[2,512,128]{2,1,0:T(8,128)(2,1)S(1)} %copy-done, ...), custom_call_target="tpu_custom_call" | custom-call | flops 134217728 | bytes 4194304 | tf_op jit(solution)/shard_map/first/pallas_call | solution.py:229
  15.7 0.0 collective-permute-done.2.d1
  15.8 2.7 %collective-permute-done.1.d2 = bf16[2,512,128]{2,1,0:T(8,128)(2,1)S(1)} collective-permute-done((bf16[2,512,128]{2,1,0:T(8,128)(2,1)}, bf16[2,512,128]{2,1,0:T(8,128)(2,1)S(1)}, u32[]{:S(2)}, u32[]{:S(2)}) %collective-permute-start.1) | collective-permute-done | bytes 262176 | tf_op jit(solution)/shard_map/ppermute | solution.py:204
  18.5 1.1 %near.1.acc_ref = f32[2,128,512]{2,1,0:T(8,128)S(1)} custom-call(s32[2]{0:T(128)S(1)} %copy-done.2, bf16[2,512,128]{2,1,0:T(8,128)(2,1)S(1)} %collective-permute-done.1.d2, bf16[2,512,128]{2,1,0:T(8,128)(2,1)S(1)} %collective-permute-done.2.d1, f32[2,128,512]{2,1,0:T(8,128)S(1)} %get-tuple-element.15.acc_ref, bf16[2,2048,512]{2,1,0:T(8,128)(2,1)S(1)} %get-tuple-element.16.fac), custom_call_target="tpu_custom_call" | custom-call | flops 268435456 | bytes 4194304 | tf_op jit(solution)/shard_map/near/pallas_call | solution.py:246
  19.5 4.3 %collective-permute-done.d3 = bf16[2,512,128]{2,1,0:T(8,128)(2,1)S(1)} collective-permute-done((bf16[2,512,128]{2,1,0:T(8,128)(2,1)}, bf16[2,512,128]{2,1,0:T(8,128)(2,1)S(1)}, u32[]{:S(2)}, u32[]{:S(2)}) %collective-permute-start) | collective-permute-done | bytes 262176 | tf_op jit(solution)/shard_map/ppermute | solution.py:204
  23.9 2.8 %traces.1 = (bf16[832,128]{1,0:T(8,128)(2,1)S(1)}, bf16[960,128]{1,0:T(8,128)(2,1)S(1)}, bf16[960,128]{1,0:T(8,128)(2,1)S(1)}, bf16[960,128]{1,0:T(8,128)(2,1)S(1)}) custom-call(s32[2]{0:T(128)S(1)} %copy-done.2, bf16[2,512,128]{2,1,0:T(8,128)(2,1)S(1)} %collective-permute-done.d3, f32[2,128,512]{2,1,0:T(8,128)S(1)} %near.1.acc_ref, ...), custom_call_target="tpu_custom_call" | custom-call | flops 1073741824 | bytes 8388608 | tf_op jit(solution)/shard_map/traces/pallas_call | solution.py:260
  26.7 1.9 %collective-permute-start.3 = (bf16[960,128]{1,0:T(8,128)(2,1)S(1)}, bf16[960,128]{1,0:T(8,128)(2,1)S(1)}, u32[]{:S(2)}, u32[]{:S(2)}) collective-permute-start(bf16[960,128]{1,0:T(8,128)(2,1)S(1)} %get-tuple-element.18), channel_id=1, source_target_pairs={{0,2},{1,3},{2,0},{3,1},{4,6},{5,7},{6,4},{7,5},{8,10},{9,11},{10,... | collective-permute-start | bytes 737288 | tf_op jit(solution)/shard_map/ppermute | solution.py:204
  28.6 3.0 %collective-permute-start.4 = (bf16[960,128]{1,0:T(8,128)(2,1)S(1)}, bf16[960,128]{1,0:T(8,128)(2,1)S(1)}, u32[]{:S(2)}, u32[]{:S(2)}) collective-permute-start(bf16[960,128]{1,0:T(8,128)(2,1)S(1)} %get-tuple-element.19), channel_id=1, source_target_pairs={{0,1},{1,0},{2,3},{3,2},{4,5},{5,4},{6,7},{7,6},{8,9},{9,8},{10,11... | collective-permute-start | bytes 737288 | tf_op jit(solution)/shard_map/ppermute | solution.py:204
  31.6 4.9 %collective-permute-start.5 = (bf16[960,128]{1,0:T(8,128)(2,1)S(1)}, bf16[960,128]{1,0:T(8,128)(2,1)S(1)}, u32[]{:S(2)}, u32[]{:S(2)}) collective-permute-start(bf16[960,128]{1,0:T(8,128)(2,1)S(1)} %get-tuple-element.20), channel_id=1, source_target_pairs={{0,3},{1,2},{2,1},{3,0},{4,7},{5,6},{6,5},{7,4},{8,11},{9,10},{10,... | collective-permute-start | bytes 737288 | tf_op jit(solution)/shard_map/ppermute | solution.py:204
  36.5 0.1 copy.13
  36.7 2.2 %collective-permute-done.3.a2 = bf16[960,128]{1,0:T(8,128)(2,1)S(1)} collective-permute-done((bf16[960,128]{1,0:T(8,128)(2,1)S(1)}, bf16[960,128]{1,0:T(8,128)(2,1)S(1)}, u32[]{:S(2)}, u32[]{:S(2)}) %collective-permute-start.3) | collective-permute-done | bytes 245792 | tf_op jit(solution)/shard_map/ppermute | solution.py:204
  38.9 1.8 %collective-permute-done.4.a1 = bf16[960,128]{1,0:T(8,128)(2,1)S(1)} collective-permute-done((bf16[960,128]{1,0:T(8,128)(2,1)S(1)}, bf16[960,128]{1,0:T(8,128)(2,1)S(1)}, u32[]{:S(2)}, u32[]{:S(2)}) %collective-permute-start.4) | collective-permute-done | bytes 245792 | tf_op jit(solution)/shard_map/ppermute | solution.py:204
  40.7 2.4 %collective-permute-done.5.a3 = bf16[960,128]{1,0:T(8,128)(2,1)S(1)} collective-permute-done((bf16[960,128]{1,0:T(8,128)(2,1)S(1)}, bf16[960,128]{1,0:T(8,128)(2,1)S(1)}, u32[]{:S(2)}, u32[]{:S(2)}) %collective-permute-start.5) | collective-permute-done | bytes 245792 | tf_op jit(solution)/shard_map/ppermute | solution.py:204
  43.1 1.1 %pack.1 = (bf16[1280,128]{1,0:T(8,128)(2,1)S(1)}, bf16[4,32,1024]{2,1,0:T(8,128)(2,1)S(1)}) custom-call(s32[2]{0:T(128)S(1)} %copy-done.2, s32[2,128]{1,0:T(2,128)S(1)} %copy-done.3, s32[2,128]{1,0:T(2,128)S(1)} %copy-done.4, f32[128,128]{1,0:T(8,128)S(1)} %get-tuple-element.14.diag_ref, bf16[128,128]{1,0:T(8,128)(2,1)S(1)} %bitcast.22, ...), custom_call_target="tpu_custom_call" | custom-call | tf_op jit(solution)/shard_map/pack/pallas_call | solution.py:277
  44.2 43.9 %all_to_all.10 = bf16[128,5,2,128]{3,2,1,0:T(2,128)(2,1)S(1)} all-to-all(bf16[128,5,2,128]{3,2,1,0:T(2,128)(2,1)S(1)} %bitcast.17), channel_id=1, replica_groups=mesh['sub'=128,'blk'=4] {'sub'}, dimensions={0} | all-to-all | bytes 655360 | tf_op jit(solution)/shard_map/all_to_all | solution.py:290
  88.1 0.6 interior.1
  88.7 8.3 %all_to_all.11 = bf16[4,32,128]{2,1,0:T(8,128)(2,1)S(1)} all-to-all(bf16[4,32,128]{2,1,0:T(8,128)(2,1)S(1)} %interior.1), channel_id=1, replica_groups=mesh['sub'=128,'blk'=4] {'blk'}, dimensions={0} | all-to-all | bytes 65536 | tf_op jit(solution)/shard_map/all_to_all | solution.py:308
  97.0 0.6 reduce_sum.12
Async XLA Ops:
  0.0 12.9 %copy-start = (bf16[2,512,128]{2,1,0:T(8,128)(2,1)S(1)}, bf16[2,512,128]{2,1,0:T(8,128)(2,1)}, u32[]{:S(2)}) copy-start(bf16[2,512,128]{2,1,0:T(8,128)(2,1)} %d0.1) | copy-start | bytes 786436
  0.0 12.9 %copy-start.2 = (s32[2]{0:T(128)S(1)}, s32[2]{0:T(128)}, u32[]{:S(2)}) copy-start(s32[2]{0:T(128)} %blocks.7) | copy-start | bytes 28
  0.0 12.9 %copy-start.4 = (s32[2,128]{1,0:T(2,128)S(1)}, s32[2,128]{1,0:T(2,128)}, u32[]{:S(2)}) copy-start(s32[2,128]{1,0:T(2,128)} %lane_ref.3) | copy-start | bytes 3076
  0.0 12.9 %copy-start.3 = (s32[2,128]{1,0:T(2,128)S(1)}, s32[2,128]{1,0:T(2,128)}, u32[]{:S(2)}) copy-start(s32[2,128]{1,0:T(2,128)} %device_ref.3) | copy-start | bytes 3076
  0.0 12.9 %copy-start.1 = (bf16[2,128,16]{1,2,0:T(8,128)(2,1)S(1)}, bf16[2,128,16]{1,2,0:T(8,128)(2,1)}, u32[]{:S(2)}) copy-start(bf16[2,128,16]{1,2,0:T(8,128)(2,1)} %param.10) | copy-start | bytes 24580
  0.0 15.7 %collective-permute-start.2 = (bf16[2,512,128]{2,1,0:T(8,128)(2,1)}, bf16[2,512,128]{2,1,0:T(8,128)(2,1)S(1)}, u32[]{:S(2)}, u32[]{:S(2)}) collective-permute-start(bf16[2,512,128]{2,1,0:T(8,128)(2,1)} %d0.1), channel_id=1, source_target_pairs={{0,1},{1,0},{2,3},{3,2},{4,5},{5,4},{6,7},{7,6},{8,9},{9,8},{10,11... | collective-permute-start | bytes 786440 | tf_op jit(solution)/shard_map/ppermute | solution.py:204
  3.7 14.8 %collective-permute-start.1 = (bf16[2,512,128]{2,1,0:T(8,128)(2,1)}, bf16[2,512,128]{2,1,0:T(8,128)(2,1)S(1)}, u32[]{:S(2)}, u32[]{:S(2)}) collective-permute-start(bf16[2,512,128]{2,1,0:T(8,128)(2,1)} %d0.1), channel_id=1, source_target_pairs={{0,2},{1,3},{2,0},{3,1},{4,6},{5,7},{6,4},{7,5},{8,10},{9,11},{10,... | collective-permute-start | bytes 786440 | tf_op jit(solution)/shard_map/ppermute | solution.py:204
  8.5 15.4 %collective-permute-start = (bf16[2,512,128]{2,1,0:T(8,128)(2,1)}, bf16[2,512,128]{2,1,0:T(8,128)(2,1)S(1)}, u32[]{:S(2)}, u32[]{:S(2)}) collective-permute-start(bf16[2,512,128]{2,1,0:T(8,128)(2,1)} %d0.1), channel_id=1, source_target_pairs={{0,3},{1,2},{2,1},{3,0},{4,7},{5,6},{6,5},{7,4},{8,11},{9,10},{10,... | collective-permute-start | bytes 786440 | tf_op jit(solution)/shard_map/ppermute | solution.py:204
  26.7 12.2 %collective-permute-start.3 = (bf16[960,128]{1,0:T(8,128)(2,1)S(1)}, bf16[960,128]{1,0:T(8,128)(2,1)S(1)}, u32[]{:S(2)}, u32[]{:S(2)}) collective-permute-start(bf16[960,128]{1,0:T(8,128)(2,1)S(1)} %get-tuple-element.18), channel_id=1, source_target_pairs={{0,2},{1,3},{2,0},{3,1},{4,6},{5,7},{6,4},{7,5},{8,10},{9,11},{10,... | collective-permute-start | bytes 737288 | tf_op jit(solution)/shard_map/ppermute | solution.py:204
  28.6 12.1 %collective-permute-start.4 = (bf16[960,128]{1,0:T(8,128)(2,1)S(1)}, bf16[960,128]{1,0:T(8,128)(2,1)S(1)}, u32[]{:S(2)}, u32[]{:S(2)}) collective-permute-start(bf16[960,128]{1,0:T(8,128)(2,1)S(1)} %get-tuple-element.19), channel_id=1, source_target_pairs={{0,1},{1,0},{2,3},{3,2},{4,5},{5,4},{6,7},{7,6},{8,9},{9,8},{10,11... | collective-permute-start | bytes 737288 | tf_op jit(solution)/shard_map/ppermute | solution.py:204
  31.6 11.5 %collective-permute-start.5 = (bf16[960,128]{1,0:T(8,128)(2,1)S(1)}, bf16[960,128]{1,0:T(8,128)(2,1)S(1)}, u32[]{:S(2)}, u32[]{:S(2)}) collective-permute-start(bf16[960,128]{1,0:T(8,128)(2,1)S(1)} %get-tuple-element.20), channel_id=1, source_target_pairs={{0,3},{1,2},{2,1},{3,0},{4,7},{5,6},{6,5},{7,4},{8,11},{9,10},{10,... | collective-permute-start | bytes 737288 | tf_op jit(solution)/shard_map/ppermute | solution.py:204

commit v2 on v1

--- a/solution.py
+++ b/solution.py
@@ -92,11 +92,11 @@
             copies[s, j].wait()
 
 
-def near_kernel(blocks, d2, d1, acc_ref, fac, out_ref):
+def near_kernel(blocks, d2, d3, acc_ref, fac, out_ref):
     offsets = row_offsets(lax.axis_index("blk"), fac.shape[2])
     accs = products(
         blocks,
-        ((d2, 2), (d1, 1)),
+        ((d2, 2), (d3, 3)),
         fac,
         offsets,
         [acc_ref[s] for s in range(fac.shape[0])],
@@ -106,12 +106,12 @@
         out_ref[s] = accs[s]
 
 
-def traces_kernel(blocks, d3, acc_ref, fac, c1, c2, c3, o0, o1, o2, o3, wide):
+def traces_kernel(blocks, d1, acc_ref, fac, c1, c2, c3, o0, o1, o2, o3, wide):
     subs, order, quarter = fac.shape
     here = lax.axis_index("blk")
     offsets = row_offsets(here, quarter)
     accs = products(
-        blocks, ((d3, 3),), fac, offsets, [acc_ref[s] for s in range(subs)], lambda s, j: None
+        blocks, ((d1, 1),), fac, offsets, [acc_ref[s] for s in range(subs)], lambda s, j: None
     )
     start = jnp.int32(0)
     for s in range(subs):
@@ -253,7 +253,7 @@
             flops=4 * subs * quarter * quarter * columns, bytes_accessed=4 << 20, transcendentals=0
         ),
         name="near",
-    )(blocks, d2, d1, acc, fac)
+    )(blocks, d2, d3, acc, fac)
 
     count = PART * FACES
     piece = jax.ShapeDtypeStruct((count + extra, columns), BF16)
@@ -268,7 +268,7 @@
             flops=4 * subs * order * quarter * columns, bytes_accessed=8 << 20, transcendentals=0
         ),
         name="traces",
-    )(blocks, d3, acc, fac, turned(1), turned(2), turned(3))
+    )(blocks, d1, acc, fac, turned(1), turned(2), turned(3))
 
     a2 = swap(o2, 2)
     a1 = swap(o1, 1)

time: 98 us -> 94.6 us (0.965)
  waiting for transfers between devices: 13.5 us -> 10.4 us
    ppermute x6, waiting for transfers between devices: 13.5 us -> 10.4 us  [swap(): return lax.ppermute(x, 'blk', [(i, i ^ j) for i in range(BLK)])]
  transfers between devices with their start and end apart: 6 -> 6, of which waited for: 5 -> 6; matrix products, arithmetic and copies ran while one was open for 2% -> 2% of each run, Pallas kernels for 4% -> 4%
where the time goes in v2:
time: 94.6 us; the launch traced here: 94.3 us
  blocking collectives  52.5 us (55%)
  starting transfers between devices  19.9 us (21%)
  waiting for transfers between devices  10.4 us (11%)
  Pallas kernels  8.32 us (9%)
  local copies, waits for them, and re-layouts  2.38 us (3%)
    all_to_all x1, blocking collectives, body(): lax.all_to_all(pay.reshape(peers, PAY // 2, 2, columns), 'sub', split_axi...  43.9 us
    ppermute x6, starting transfers between devices, swap(): return lax.ppermute(x, 'blk', [(i, i ^ j) for i in range(BLK)])  19.9 us
    ppermute x6, waiting for transfers between devices, swap(): return lax.ppermute(x, 'blk', [(i, i ^ j) for i in range(BLK)])  10.4 us
    all_to_all x1, blocking collectives, body(): parts = lax.all_to_all(part, 'blk', split_axis=0, concat_axis=0, tiled=True)  8.6 us
    pallas_call x1, Pallas kernels, body(): pl.pallas_call(first_kernel, out_shape=[jax.ShapeDtypeStruct(factor.shape...  2.81 us
    pallas_call x1, Pallas kernels, body(): pl.pallas_call(traces_kernel, out_shape=[jax.ShapeDtypeStruct((count, col...  2.78 us
  transfers between devices with their start and end apart: 6, of which 6 were waited for; matrix products, arithmetic and copies ran while one was open for 2% of the time, Pallas kernels for 4%

profile of v2, /device:TPU:6, one launch (start us, length us, event | category | flops | bytes accessed | tf_op | source)
XLA Modules:
  0.0 94.3 jit_solution(13661814940047192278)
XLA Ops:
  0.0 0.0 copy-start
  0.0 0.0 copy-start.2
  0.0 0.0 copy-start.4
  0.0 0.0 copy-start.3
  0.0 0.0 copy-start.1
  0.0 5.1 %collective-permute-start.2 = (bf16[2,512,128]{2,1,0:T(8,128)(2,1)}, bf16[2,512,128]{2,1,0:T(8,128)(2,1)S(1)}, u32[]{:S(2)}, u32[]{:S(2)}) collective-permute-start(bf16[2,512,128]{2,1,0:T(8,128)(2,1)} %d0.1), channel_id=1, source_target_pairs={{0,3},{1,2},{2,1},{3,0},{4,7},{5,6},{6,5},{7,4},{8,11},{9,10},{10,... | collective-permute-start | bytes 786440 | tf_op jit(solution)/shard_map/ppermute | solution.py:204
  5.1 2.5 %collective-permute-start.1 = (bf16[2,512,128]{2,1,0:T(8,128)(2,1)}, bf16[2,512,128]{2,1,0:T(8,128)(2,1)S(1)}, u32[]{:S(2)}, u32[]{:S(2)}) collective-permute-start(bf16[2,512,128]{2,1,0:T(8,128)(2,1)} %d0.1), channel_id=1, source_target_pairs={{0,2},{1,3},{2,0},{3,1},{4,6},{5,7},{6,4},{7,5},{8,10},{9,11},{10,... | collective-permute-start | bytes 786440 | tf_op jit(solution)/shard_map/ppermute | solution.py:204
  7.6 2.4 %collective-permute-start = (bf16[2,512,128]{2,1,0:T(8,128)(2,1)}, bf16[2,512,128]{2,1,0:T(8,128)(2,1)S(1)}, u32[]{:S(2)}, u32[]{:S(2)}) collective-permute-start(bf16[2,512,128]{2,1,0:T(8,128)(2,1)} %d0.1), channel_id=1, source_target_pairs={{0,1},{1,0},{2,3},{3,2},{4,5},{5,4},{6,7},{7,6},{8,9},{9,8},{10,11... | collective-permute-start | bytes 786440 | tf_op jit(solution)/shard_map/ppermute | solution.py:204
  10.0 1.4 %copy.12 = bf16[2,16,2048]{1,2,0:T(8,128)(2,1)S(1)} copy(bf16[2,16,2048]{2,1,0:T(8,128)(2,1)} %param.11) | data formatting | bytes 262144 | tf_op args[3]
  11.4 0.4 dynamic-slice_bitcast_fusion
  11.8 0.1 copy.16
  11.9 0.2 copy.15
  12.1 0.2 copy.14
  12.3 0.0 copy-done
  12.3 0.0 copy-done.2
  12.3 0.0 copy-done.4
  12.3 0.0 copy-done.3
  12.3 0.0 copy-done.1
  12.3 2.8 %first.1 = (bf16[2,2048,512]{2,1,0:T(8,128)(2,1)S(1)}, f32[2,128,512]{2,1,0:T(8,128)S(1)}, f32[128,128]{1,0:T(8,128)S(1)}) custom-call(s32[2]{0:T(128)S(1)} %copy-done.2, s32[2,128]{1,0:T(2,128)S(1)} %copy-done.3, s32[2,128]{1,0:T(2,128)S(1)} %copy-done.4, bf16[2,16,128]{2,1,0:T(8,128)(2,1)S(1)} %bitcast.23, bf16[2,512,128]{2,1,0:T(8,128)(2,1)S(1)} %copy-done, ...), custom_call_target="tpu_custom_call" | custom-call | flops 134217728 | bytes 4194304 | tf_op jit(solution)/shard_map/first/pallas_call | solution.py:229
  15.1 1.4 %collective-permute-done.2.d3 = bf16[2,512,128]{2,1,0:T(8,128)(2,1)S(1)} collective-permute-done((bf16[2,512,128]{2,1,0:T(8,128)(2,1)}, bf16[2,512,128]{2,1,0:T(8,128)(2,1)S(1)}, u32[]{:S(2)}, u32[]{:S(2)}) %collective-permute-start.2) | collective-permute-done | bytes 262176 | tf_op jit(solution)/shard_map/ppermute | solution.py:204
  16.6 1.3 %collective-permute-done.1.d2 = bf16[2,512,128]{2,1,0:T(8,128)(2,1)S(1)} collective-permute-done((bf16[2,512,128]{2,1,0:T(8,128)(2,1)}, bf16[2,512,128]{2,1,0:T(8,128)(2,1)S(1)}, u32[]{:S(2)}, u32[]{:S(2)}) %collective-permute-start.1) | collective-permute-done | bytes 262176 | tf_op jit(solution)/shard_map/ppermute | solution.py:204
  17.9 1.1 %near.1.acc_ref = f32[2,128,512]{2,1,0:T(8,128)S(1)} custom-call(s32[2]{0:T(128)S(1)} %copy-done.2, bf16[2,512,128]{2,1,0:T(8,128)(2,1)S(1)} %collective-permute-done.1.d2, bf16[2,512,128]{2,1,0:T(8,128)(2,1)S(1)} %collective-permute-done.2.d3, f32[2,128,512]{2,1,0:T(8,128)S(1)} %get-tuple-element.15.acc_ref, bf16[2,2048,512]{2,1,0:T(8,128)(2,1)S(1)} %get-tuple-element.16.fac), custom_call_target="tpu_custom_call" | custom-call | flops 268435456 | bytes 4194304 | tf_op jit(solution)/shard_map/near/pallas_call | solution.py:246
  18.9 0.8 collective-permute-done.d1
  19.7 2.8 %traces.1 = (bf16[832,128]{1,0:T(8,128)(2,1)S(1)}, bf16[960,128]{1,0:T(8,128)(2,1)S(1)}, bf16[960,128]{1,0:T(8,128)(2,1)S(1)}, bf16[960,128]{1,0:T(8,128)(2,1)S(1)}) custom-call(s32[2]{0:T(128)S(1)} %copy-done.2, bf16[2,512,128]{2,1,0:T(8,128)(2,1)S(1)} %collective-permute-done.d1, f32[2,128,512]{2,1,0:T(8,128)S(1)} %near.1.acc_ref, ...), custom_call_target="tpu_custom_call" | custom-call | flops 1073741824 | bytes 8388608 | tf_op jit(solution)/shard_map/traces/pallas_call | solution.py:260
  22.5 5.0 %collective-permute-start.3 = (bf16[960,128]{1,0:T(8,128)(2,1)S(1)}, bf16[960,128]{1,0:T(8,128)(2,1)S(1)}, u32[]{:S(2)}, u32[]{:S(2)}) collective-permute-start(bf16[960,128]{1,0:T(8,128)(2,1)S(1)} %get-tuple-element.18), channel_id=1, source_target_pairs={{0,2},{1,3},{2,0},{3,1},{4,6},{5,7},{6,4},{7,5},{8,10},{9,11},{10,... | collective-permute-start | bytes 737288 | tf_op jit(solution)/shard_map/ppermute | solution.py:204
  27.6 2.6 %collective-permute-start.4 = (bf16[960,128]{1,0:T(8,128)(2,1)S(1)}, bf16[960,128]{1,0:T(8,128)(2,1)S(1)}, u32[]{:S(2)}, u32[]{:S(2)}) collective-permute-start(bf16[960,128]{1,0:T(8,128)(2,1)S(1)} %get-tuple-element.19), channel_id=1, source_target_pairs={{0,1},{1,0},{2,3},{3,2},{4,5},{5,4},{6,7},{7,6},{8,9},{9,8},{10,11... | collective-permute-start | bytes 737288 | tf_op jit(solution)/shard_map/ppermute | solution.py:204
  30.2 2.3 %collective-permute-start.5 = (bf16[960,128]{1,0:T(8,128)(2,1)S(1)}, bf16[960,128]{1,0:T(8,128)(2,1)S(1)}, u32[]{:S(2)}, u32[]{:S(2)}) collective-permute-start(bf16[960,128]{1,0:T(8,128)(2,1)S(1)} %get-tuple-element.20), channel_id=1, source_target_pairs={{0,3},{1,2},{2,1},{3,0},{4,7},{5,6},{6,5},{7,4},{8,11},{9,10},{10,... | collective-permute-start | bytes 737288 | tf_op jit(solution)/shard_map/ppermute | solution.py:204
  32.5 0.1 copy.13
  32.6 1.6 %collective-permute-done.3.a2 = bf16[960,128]{1,0:T(8,128)(2,1)S(1)} collective-permute-done((bf16[960,128]{1,0:T(8,128)(2,1)S(1)}, bf16[960,128]{1,0:T(8,128)(2,1)S(1)}, u32[]{:S(2)}, u32[]{:S(2)}) %collective-permute-start.3) | collective-permute-done | bytes 245792 | tf_op jit(solution)/shard_map/ppermute | solution.py:204
  34.2 3.9 %collective-permute-done.4.a1 = bf16[960,128]{1,0:T(8,128)(2,1)S(1)} collective-permute-done((bf16[960,128]{1,0:T(8,128)(2,1)S(1)}, bf16[960,128]{1,0:T(8,128)(2,1)S(1)}, u32[]{:S(2)}, u32[]{:S(2)}) %collective-permute-start.4) | collective-permute-done | bytes 245792 | tf_op jit(solution)/shard_map/ppermute | solution.py:204
  38.1 1.4 %collective-permute-done.5.a3 = bf16[960,128]{1,0:T(8,128)(2,1)S(1)} collective-permute-done((bf16[960,128]{1,0:T(8,128)(2,1)S(1)}, bf16[960,128]{1,0:T(8,128)(2,1)S(1)}, u32[]{:S(2)}, u32[]{:S(2)}) %collective-permute-start.5) | collective-permute-done | bytes 245792 | tf_op jit(solution)/shard_map/ppermute | solution.py:204
  39.5 1.1 %pack.1 = (bf16[1280,128]{1,0:T(8,128)(2,1)S(1)}, bf16[4,32,1024]{2,1,0:T(8,128)(2,1)S(1)}) custom-call(s32[2]{0:T(128)S(1)} %copy-done.2, s32[2,128]{1,0:T(2,128)S(1)} %copy-done.3, s32[2,128]{1,0:T(2,128)S(1)} %copy-done.4, f32[128,128]{1,0:T(8,128)S(1)} %get-tuple-element.14.diag_ref, bf16[128,128]{1,0:T(8,128)(2,1)S(1)} %bitcast.22, ...), custom_call_target="tpu_custom_call" | custom-call | tf_op jit(solution)/shard_map/pack/pallas_call | solution.py:277
  40.5 43.9 %all_to_all.10 = bf16[128,5,2,128]{3,2,1,0:T(2,128)(2,1)S(1)} all-to-all(bf16[128,5,2,128]{3,2,1,0:T(2,128)(2,1)S(1)} %bitcast.17), channel_id=1, replica_groups=mesh['sub'=128,'blk'=4] {'sub'}, dimensions={0} | all-to-all | bytes 655360 | tf_op jit(solution)/shard_map/all_to_all | solution.py:290
  84.4 0.6 interior.1
  85.1 8.6 %all_to_all.11 = bf16[4,32,128]{2,1,0:T(8,128)(2,1)S(1)} all-to-all(bf16[4,32,128]{2,1,0:T(8,128)(2,1)S(1)} %interior.1), channel_id=1, replica_groups=mesh['sub'=128,'blk'=4] {'blk'}, dimensions={0} | all-to-all | bytes 65536 | tf_op jit(solution)/shard_map/all_to_all | solution.py:308
  93.7 0.6 reduce_sum.12
Async XLA Ops:
  0.0 12.3 %copy-start = (bf16[2,512,128]{2,1,0:T(8,128)(2,1)S(1)}, bf16[2,512,128]{2,1,0:T(8,128)(2,1)}, u32[]{:S(2)}) copy-start(bf16[2,512,128]{2,1,0:T(8,128)(2,1)} %d0.1) | copy-start | bytes 786436
  0.0 12.3 %copy-start.2 = (s32[2]{0:T(128)S(1)}, s32[2]{0:T(128)}, u32[]{:S(2)}) copy-start(s32[2]{0:T(128)} %blocks.7) | copy-start | bytes 28
  0.0 12.3 %copy-start.4 = (s32[2,128]{1,0:T(2,128)S(1)}, s32[2,128]{1,0:T(2,128)}, u32[]{:S(2)}) copy-start(s32[2,128]{1,0:T(2,128)} %lane_ref.3) | copy-start | bytes 3076
  0.0 12.3 %copy-start.3 = (s32[2,128]{1,0:T(2,128)S(1)}, s32[2,128]{1,0:T(2,128)}, u32[]{:S(2)}) copy-start(s32[2,128]{1,0:T(2,128)} %device_ref.3) | copy-start | bytes 3076
  0.0 12.3 %copy-start.1 = (bf16[2,128,16]{1,2,0:T(8,128)(2,1)S(1)}, bf16[2,128,16]{1,2,0:T(8,128)(2,1)}, u32[]{:S(2)}) copy-start(bf16[2,128,16]{1,2,0:T(8,128)(2,1)} %param.10) | copy-start | bytes 24580
  0.0 16.5 %collective-permute-start.2 = (bf16[2,512,128]{2,1,0:T(8,128)(2,1)}, bf16[2,512,128]{2,1,0:T(8,128)(2,1)S(1)}, u32[]{:S(2)}, u32[]{:S(2)}) collective-permute-start(bf16[2,512,128]{2,1,0:T(8,128)(2,1)} %d0.1), channel_id=1, source_target_pairs={{0,3},{1,2},{2,1},{3,0},{4,7},{5,6},{6,5},{7,4},{8,11},{9,10},{10,... | collective-permute-start | bytes 786440 | tf_op jit(solution)/shard_map/ppermute | solution.py:204
  5.1 12.8 %collective-permute-start.1 = (bf16[2,512,128]{2,1,0:T(8,128)(2,1)}, bf16[2,512,128]{2,1,0:T(8,128)(2,1)S(1)}, u32[]{:S(2)}, u32[]{:S(2)}) collective-permute-start(bf16[2,512,128]{2,1,0:T(8,128)(2,1)} %d0.1), channel_id=1, source_target_pairs={{0,2},{1,3},{2,0},{3,1},{4,6},{5,7},{6,4},{7,5},{8,10},{9,11},{10,... | collective-permute-start | bytes 786440 | tf_op jit(solution)/shard_map/ppermute | solution.py:204
  7.6 12.1 %collective-permute-start = (bf16[2,512,128]{2,1,0:T(8,128)(2,1)}, bf16[2,512,128]{2,1,0:T(8,128)(2,1)S(1)}, u32[]{:S(2)}, u32[]{:S(2)}) collective-permute-start(bf16[2,512,128]{2,1,0:T(8,128)(2,1)} %d0.1), channel_id=1, source_target_pairs={{0,1},{1,0},{2,3},{3,2},{4,5},{5,4},{6,7},{7,6},{8,9},{9,8},{10,11... | collective-permute-start | bytes 786440 | tf_op jit(solution)/shard_map/ppermute | solution.py:204
  22.5 11.7 %collective-permute-start.3 = (bf16[960,128]{1,0:T(8,128)(2,1)S(1)}, bf16[960,128]{1,0:T(8,128)(2,1)S(1)}, u32[]{:S(2)}, u32[]{:S(2)}) collective-permute-start(bf16[960,128]{1,0:T(8,128)(2,1)S(1)} %get-tuple-element.18), channel_id=1, source_target_pairs={{0,2},{1,3},{2,0},{3,1},{4,6},{5,7},{6,4},{7,5},{8,10},{9,11},{10,... | collective-permute-start | bytes 737288 | tf_op jit(solution)/shard_map/ppermute | solution.py:204
  27.6 10.5 %collective-permute-start.4 = (bf16[960,128]{1,0:T(8,128)(2,1)S(1)}, bf16[960,128]{1,0:T(8,128)(2,1)S(1)}, u32[]{:S(2)}, u32[]{:S(2)}) collective-permute-start(bf16[960,128]{1,0:T(8,128)(2,1)S(1)} %get-tuple-element.19), channel_id=1, source_target_pairs={{0,1},{1,0},{2,3},{3,2},{4,5},{5,4},{6,7},{7,6},{8,9},{9,8},{10,11... | collective-permute-start | bytes 737288 | tf_op jit(solution)/shard_map/ppermute | solution.py:204
  30.2 9.3 %collective-permute-start.5 = (bf16[960,128]{1,0:T(8,128)(2,1)S(1)}, bf16[960,128]{1,0:T(8,128)(2,1)S(1)}, u32[]{:S(2)}, u32[]{:S(2)}) collective-permute-start(bf16[960,128]{1,0:T(8,128)(2,1)S(1)} %get-tuple-element.20), channel_id=1, source_target_pairs={{0,3},{1,2},{2,1},{3,0},{4,7},{5,6},{6,5},{7,4},{8,11},{9,10},{10,... | collective-permute-start | bytes 737288 | tf_op jit(solution)/shard_map/ppermute | solution.py:204
